TPU v7x, 32 devices: a whole 2x2x4 slice. The times are simulated.
32 devices in a mesh: seq: 8 (over z, x), head: 4 (over y, core).
Axes of the slice: x: 2, y: 2, z: 4, core: 2. Of those that a mesh axis runs over, the one named last changes fastest.
Arguments:
- queries: bfloat16 [4096, 5120], P('seq', 'head'), may hold values from -13 to 13, as said below
- keys: bfloat16 [4096, 1024], P('seq', 'head'), may hold values from -13 to 13, as said below
- values: bfloat16 [4096, 1024], P('seq', 'head'), may hold values from -6 to 6
- out_weight: bfloat16 [5120, 2560], P('head', 'seq'), may hold values from -0.078125 to 0.078125
- d_proj: bfloat16 [4096, 2560], P('seq', 'head'), may hold values from -6 to 6
- block_section: int32 [32], replicated, may hold values from 0 to 3, as said below
- section_parent: int32 [4], replicated, may hold values from -1 to 2, as said below
- xref_owner: int32 [384, 1], P('seq'), may hold values from 0 to 7; in each aligned block of 48 rows (0 to 47, 48 to 95, ...) at most 6 rows name the same one
- xref_block: int32 [32, 12], P('seq'), may hold values from 0 to 3
- xref_valid: int32 [32, 12], P('seq'), may hold values 0 or 1
Outputs:
- projected: bfloat16 [4096, 2560], P('seq', 'head')
- d_queries: bfloat16 [4096, 5120], P('seq', 'head')
- d_keys: bfloat16 [4096, 1024], P('seq', 'head')
- d_values: bfloat16 [4096, 1024], P('seq', 'head')
Inputs may be any that keep to these rules, and one draw needn't show every extreme that they name: `queries`: entries of order one; a few rows of larger norm. `keys`: entries of order one; a few rows of larger norm. section_parent[s] is an earlier section for s > 0, and section_parent[0] = -1. `block_section`: sections are runs of consecutive blocks, 2 to 14 blocks each, some section exactly 14; no section begins at a block whose index is a positive multiple of 4. `xref_owner`: among the 48 rows of one device, no owner is named more than 6 times; some owner exactly 6 times.
All inputs are finite; a program needn't handle non-finite values. No bound on the sum of `xref_valid` on one device may be relied on, other than what follows from the above.
Results may differ from a plain program's by a relative error of at most 0.015.
The roundings to bfloat16 on the way count: a program that leaves them out, or rounds other values in their place, can miss the bound.
Values may be sent and summed in bfloat16 or wider, within the bound.
No kernel may reach another device: no remote copies, remote signals or barrier semaphores. Data moves between devices by JAX's collectives and lax.ppermute only.
A program may use at most 192 MiB of HBM per device.

v0:
```python
import jax
import jax.numpy as jnp
from jax import lax
from jax.sharding import PartitionSpec as P

HEAD_DIMENSION = 128
BLK = 128
LOOK = 4
ANC = 2
XREF = 12
neg_large = -1e30


def passed_along(block, axis, distance):
    devices = range(lax.axis_size(axis))
    route = [(i - distance, i) for i in devices if i - distance in devices]
    return lax.ppermute(block, axis, route)


def query_layout(block, kv_heads):
    row_count = block.shape[0]
    group_size = block.shape[1] // (HEAD_DIMENSION * kv_heads)
    return block.reshape(row_count, kv_heads, group_size, HEAD_DIMENSION)


def key_layout(key_set, kv_heads):
    num_blocks, row_count, key_value_width = key_set.shape
    return key_set.reshape(num_blocks * row_count, kv_heads, HEAD_DIMENSION)


def softmax_weights(scores, allowed):
    masked = jnp.where(allowed, scores, neg_large)
    row_max = jnp.max(masked, axis=-1, keepdims=True)
    exponent = jnp.where(allowed, jnp.exp(masked - row_max), 0.0)
    return exponent / jnp.sum(exponent, axis=-1, keepdims=True)


def product(form, left, right):
    return jnp.einsum(form, left, right, preferred_element_type=jnp.float32)


def forward_block(query_block, key_set, value_set, allowed):
    kv_heads = key_set.shape[2] // HEAD_DIMENSION
    scaling = HEAD_DIMENSION ** (-0.5)
    query_heads = query_layout(query_block, kv_heads)
    key_heads = key_layout(key_set, kv_heads)
    value_heads = key_layout(value_set, kv_heads)
    scores = product("qcgd,kcd->cqgk", query_heads, key_heads) * scaling
    weights = softmax_weights(scores, allowed[None, :, None, :])
    output = product("cqgk,kcd->qcgd", weights.astype(jnp.bfloat16), value_heads)
    return output.reshape(query_block.shape[0], -1).astype(jnp.bfloat16)


def backward_block(query_block, key_set, value_set, allowed, attn, d_attn):
    kv_heads = key_set.shape[2] // HEAD_DIMENSION
    scaling = HEAD_DIMENSION ** (-0.5)
    num_blocks = key_set.shape[0]
    row_count = query_block.shape[0]
    query_heads = query_layout(query_block, kv_heads)
    key_heads = key_layout(key_set, kv_heads)
    value_heads = key_layout(value_set, kv_heads)
    scores = product("qcgd,kcd->cqgk", query_heads, key_heads) * scaling
    weights = softmax_weights(scores, allowed[None, :, None, :])
    light = weights.astype(jnp.bfloat16)
    grad_heads = query_layout(d_attn, kv_heads)
    attn_heads = query_layout(attn, kv_heads)
    delta = jnp.einsum(
        "qcgd,qcgd->cqg", grad_heads.astype(jnp.float32), attn_heads.astype(jnp.float32)
    )[..., None]
    d_weights = product("qcgd,kcd->cqgk", grad_heads, value_heads)
    d_scores = (weights * (d_weights - delta) * scaling).astype(jnp.bfloat16)
    grad_query = product("cqgk,kcd->qcgd", d_scores, key_heads)
    key_terms = product("cqgk,qcgd->kcd", d_scores, query_heads)
    value_terms = product("cqgk,qcgd->kcd", light, grad_heads)
    return (
        grad_query.reshape(row_count, -1).astype(jnp.bfloat16),
        key_terms.reshape(num_blocks, -1),
        value_terms.reshape(num_blocks, -1),
    )


def run_forward(operands):
    return forward_block(operands[0], operands[1], operands[2], operands[3])


def run_backward(operands):
    return backward_block(
        operands[0], operands[1], operands[2], operands[3], operands[4], operands[5]
    )


def on_device(
    queries,
    keys,
    values,
    out_weight,
    d_proj,
    block_section,
    section_parent,
    xref_owner,
    xref_block,
    xref_valid,
):
    seq_count = lax.axis_size("seq")
    seq_rank = lax.axis_index("seq")
    tok_local = queries.shape[0]
    blk_count = tok_local // BLK
    key_value_width = keys.shape[1]
    blk_width = BLK * key_value_width
    sections = section_parent.shape[0]
    behind = LOOK - 1
    key_count = LOOK + ANC + XREF
    first_blk = seq_rank * blk_count
    key_flat = keys.reshape(blk_count, blk_width)
    value_flat = values.reshape(blk_count, blk_width)
    section_ids = jnp.arange(sections, dtype=jnp.int32)
    my_sec = lax.dynamic_slice_in_dim(block_section, first_blk, blk_count)
    counts = jnp.sum((block_section[:, None] == section_ids[None, :]).astype(jnp.float32), axis=0)
    root_counts = jnp.sqrt(counts)
    mine = (section_ids[:, None] == my_sec[None, :]).astype(jnp.float32)
    chain = [my_sec]
    prior = chain[-1]
    chain.append(
        jnp.where(
            prior >= 0,
            jnp.sum(
                jnp.where(prior[:, None] == section_ids[None, :], section_parent[None, :], 0),
                axis=1,
            ),
            -1,
        )
    )
    ancestors = jnp.stack(chain, axis=1).reshape(-1)
    chosen_up = ancestors[:, None] == section_ids[None, :]
    prev_keys, prev_values = passed_along(
        (keys[tok_local - behind * BLK :], values[tok_local - behind * BLK :]), "seq", 1
    )
    extended_keys = jnp.concatenate([prev_keys, keys], axis=0).reshape(
        blk_count + behind, BLK, key_value_width
    )
    extended_values = jnp.concatenate([prev_values, values], axis=0).reshape(
        blk_count + behind, BLK, key_value_width
    )
    mine_light = mine.astype(jnp.bfloat16)
    part_keys = (
        jnp.dot(mine_light, key_flat, preferred_element_type=jnp.float32) / root_counts[:, None]
    )
    part_values = (
        jnp.dot(mine_light, value_flat, preferred_element_type=jnp.float32) / root_counts[:, None]
    )
    total_keys, total_values = (
        lax.psum(part_keys.astype(jnp.bfloat16), "seq").astype(jnp.float32),
        lax.psum(part_values.astype(jnp.bfloat16), "seq").astype(jnp.float32),
    )
    summary_keys = total_keys.astype(jnp.bfloat16)
    summary_values = total_values.astype(jnp.bfloat16)
    chosen_light = chosen_up.astype(jnp.bfloat16)
    up_keys = (
        jnp.dot(chosen_light, summary_keys, preferred_element_type=jnp.float32)
        .astype(jnp.bfloat16)
        .reshape(blk_count, ANC, BLK, key_value_width)
    )
    up_values = (
        jnp.dot(chosen_light, summary_values, preferred_element_type=jnp.float32)
        .astype(jnp.bfloat16)
        .reshape(blk_count, ANC, BLK, key_value_width)
    )
    owners = xref_owner.reshape(-1)
    wanted = xref_block.reshape(-1)
    slot_total = owners.shape[0]
    slot_cap = max(2, slot_total // seq_count)
    slot_order = jnp.arange(slot_total)
    slot_rank = jnp.sum(
        (owners[:, None] == owners[None, :]) & (slot_order[:, None] > slot_order[None, :]), axis=1
    )
    placed = (owners * slot_cap + slot_rank)[:, None] == jnp.arange(seq_count * slot_cap)[None, :]
    placed_light = placed.astype(jnp.bfloat16)
    request = jnp.sum(jnp.where(placed, wanted[:, None] + 1, 0), axis=0).reshape(
        seq_count, slot_cap
    )
    asked_for = lax.all_to_all(request, "seq", split_axis=0, concat_axis=0, tiled=True).reshape(-1)
    served = ((asked_for - 1)[:, None] == jnp.arange(blk_count)[None, :]).astype(jnp.bfloat16)
    all_keys, all_values = (
        lax.all_gather(keys, "seq", axis=0, tiled=True),
        lax.all_gather(values, "seq", axis=0, tiled=True),
    )
    picked = (
        (owners * blk_count + wanted)[:, None] == jnp.arange(blk_count * seq_count)[None, :]
    ).astype(jnp.bfloat16)
    ref_keys = jnp.dot(
        picked,
        all_keys.reshape(blk_count * seq_count, blk_width),
        preferred_element_type=jnp.float32,
    )
    ref_values = jnp.dot(
        picked,
        all_values.reshape(blk_count * seq_count, blk_width),
        preferred_element_type=jnp.float32,
    )
    ref_keys = ref_keys.astype(jnp.bfloat16).reshape(blk_count, XREF, BLK, key_value_width)
    ref_values = ref_values.astype(jnp.bfloat16).reshape(blk_count, XREF, BLK, key_value_width)
    window_keys = jnp.stack(
        [extended_keys[offset : offset + blk_count] for offset in range(LOOK)], axis=1
    )
    window_values = jnp.stack(
        [extended_values[offset : offset + blk_count] for offset in range(LOOK)], axis=1
    )
    key_sets = jnp.concatenate([window_keys, up_keys, ref_keys], axis=1)
    value_sets = jnp.concatenate([window_values, up_values, ref_values], axis=1)
    positions = jnp.arange(BLK)
    causal = positions[None, :] <= positions[:, None]
    is_last = jnp.arange(LOOK) == LOOK - 1
    padded_sec = jnp.concatenate([jnp.full((behind,), -1, jnp.int32), block_section])
    extended_sec = lax.dynamic_slice_in_dim(padded_sec, first_blk, blk_count + behind)
    window_sec = jnp.stack(
        [extended_sec[offset : offset + blk_count] for offset in range(LOOK)], axis=1
    )
    own_ok = window_sec == my_sec[:, None]
    own_allowed = own_ok[:, None, :, None] & (
        jnp.logical_not(is_last)[None, None, :, None] | causal[None, :, None, :]
    )
    up_allowed = jnp.broadcast_to(
        (ancestors >= 0).reshape(blk_count, ANC)[:, None, :, None], (blk_count, BLK, ANC, BLK)
    )
    ref_allowed = jnp.broadcast_to((xref_valid > 0)[:, None, :, None], (blk_count, BLK, XREF, BLK))
    allowed = jnp.concatenate([own_allowed, up_allowed, ref_allowed], axis=2).reshape(
        blk_count, BLK, key_count * BLK
    )
    query_blocks = queries.reshape(blk_count, BLK, -1)
    attn_blocks = lax.map(run_forward, (query_blocks, key_sets, value_sets, allowed))
    attn = attn_blocks.reshape(tok_local, -1)
    d_full = lax.all_gather(d_proj, "head", axis=1, tiled=True)
    partials = jnp.dot(
        attn,
        lax.all_gather(out_weight, "seq", axis=1, tiled=True),
        preferred_element_type=jnp.float32,
    )
    d_attn = lax.dot_general(
        d_full,
        lax.all_gather(out_weight, "seq", axis=1, tiled=True),
        (((1,), (1,)), ((), ())),
        preferred_element_type=jnp.float32,
    ).astype(jnp.bfloat16)
    projected = lax.psum_scatter(
        partials.astype(jnp.bfloat16), "head", scatter_dimension=1, tiled=True
    )
    grad_queries, key_terms, value_terms = lax.map(
        run_backward,
        (
            query_blocks,
            key_sets,
            value_sets,
            allowed,
            attn_blocks,
            d_attn.reshape(blk_count, BLK, -1),
        ),
    )

    def spread(terms):
        extended = jnp.zeros((blk_count + behind, blk_width), jnp.float32)
        for offset in range(LOOK):
            extended = extended.at[offset : offset + blk_count].add(terms[:, offset])
        return extended

    extended_dk = spread(key_terms)
    extended_dv = spread(value_terms)
    next_dk, next_dv = (
        passed_along(extended_dk[:behind].astype(jnp.bfloat16), "seq", -1).astype(jnp.float32),
        passed_along(extended_dv[:behind].astype(jnp.bfloat16), "seq", -1).astype(jnp.float32),
    )
    own_dk = extended_dk[behind:] + jnp.pad(next_dk, ((blk_count - behind, 0), (0, 0)))
    own_dv = extended_dv[behind:] + jnp.pad(next_dv, ((blk_count - behind, 0), (0, 0)))
    chosen_float = chosen_up.T.astype(jnp.float32)
    section_dk = jnp.dot(
        chosen_float,
        key_terms[:, LOOK : LOOK + ANC].reshape(blk_count * ANC, blk_width),
        precision=lax.Precision.HIGHEST,
    )
    section_dv = jnp.dot(
        chosen_float,
        value_terms[:, LOOK : LOOK + ANC].reshape(blk_count * ANC, blk_width),
        precision=lax.Precision.HIGHEST,
    )
    summed_dk, summed_dv = (
        lax.psum(section_dk.astype(jnp.bfloat16), "seq").astype(jnp.float32),
        lax.psum(section_dv.astype(jnp.bfloat16), "seq").astype(jnp.float32),
    )
    spread_down = (mine / root_counts[:, None]).T
    up_dk = jnp.dot(spread_down, summed_dk, precision=lax.Precision.HIGHEST)
    up_dv = jnp.dot(spread_down, summed_dv, precision=lax.Precision.HIGHEST)
    slot_dk_light = (
        key_terms[:, LOOK + ANC :].reshape(blk_count * XREF, blk_width).astype(jnp.bfloat16)
    )
    slot_dv_light = (
        value_terms[:, LOOK + ANC :].reshape(blk_count * XREF, blk_width).astype(jnp.bfloat16)
    )
    placed_back = placed_light.T
    slot_dk = (
        jnp.dot(placed_back, slot_dk_light, preferred_element_type=jnp.float32)
        .astype(jnp.bfloat16)
        .reshape(seq_count, slot_cap, blk_width)
    )
    slot_dv = (
        jnp.dot(placed_back, slot_dv_light, preferred_element_type=jnp.float32)
        .astype(jnp.bfloat16)
        .reshape(seq_count, slot_cap, blk_width)
    )
    back_dk, back_dv = (
        lax.all_to_all(slot_dk, "seq", split_axis=0, concat_axis=0, tiled=True),
        lax.all_to_all(slot_dv, "seq", split_axis=0, concat_axis=0, tiled=True),
    )
    served_back = served.T
    ref_dk = jnp.dot(
        served_back,
        back_dk.reshape(seq_count * slot_cap, blk_width),
        preferred_element_type=jnp.float32,
    )
    ref_dv = jnp.dot(
        served_back,
        back_dv.reshape(seq_count * slot_cap, blk_width),
        preferred_element_type=jnp.float32,
    )
    d_keys = (own_dk + up_dk + ref_dk).astype(jnp.bfloat16).reshape(tok_local, key_value_width)
    d_values = (own_dv + up_dv + ref_dv).astype(jnp.bfloat16).reshape(tok_local, key_value_width)
    return (projected, grad_queries.reshape(tok_local, -1), d_keys, d_values)


def solution(mesh):
    placed = (
        P("seq", "head"),
        P("seq", "head"),
        P("seq", "head"),
        P("head", "seq"),
        P("seq", "head"),
        P(),
        P(),
        P("seq", None),
        P("seq", None),
        P("seq", None),
    )
    return jax.shard_map(
        on_device,
        mesh=mesh,
        in_specs=placed,
        out_specs=(P("seq", "head"), P("seq", "head"), P("seq", "head"), P("seq", "head")),
        check_vma=False,
    )
```

profile of v0, /device:TPU:0, one launch (start us, length us, event | category | flops | bytes accessed | tf_op | source)
XLA Modules:
  0.0 916.1 jit_solution(16726008169949510569)
XLA Ops:
  15.9 5.5 collective-permute-start
  25.4 4.8 all-to-all-start
  45.3 45.7 %all-reduce.12.cloned.1.call-done = (bf16[4,32768]{1,0:T(4,128)(2,1)}, bf16[4,32768]{1,0:T(4,128)(2,1)}) async-done(((bf16[4,32768]{1,0:T(4,128)(2,1)}, bf16[4,32768]{1,0:T(4,128)(2,1)}), (bf16[4,32768]{1,0:T(4,128)(2,1)}, bf16[4,32768]{1,0:T(4,128)(2,1)})) %all-reduce.12.cloned.1.call-update) | async-done | bytes 524304 | tf_op jit(solution)/shard_map/psum | solution.py:153
  95.5 45.9 %all-gather.5.cloned.1.call-done = bf16[4096,256]{1,0:T(8,128)(2,1)} async-done(((bf16[512,256]{1,0:T(8,128)(2,1)}), bf16[4096,256]{1,0:T(8,128)(2,1)}) %all-gather.5.cloned.1.call-update) | async-done | bytes 2097168 | tf_op jit(solution)/shard_map/all_gather | solution.py:185
  146.0 45.1 %all-gather.7.cloned.1.call-done = bf16[4096,256]{1,0:T(8,128)(2,1)} async-done(((bf16[512,256]{1,0:T(8,128)(2,1)}), bf16[4096,256]{1,0:T(8,128)(2,1)}) %all-gather.7.cloned.1.call-update) | async-done | bytes 2097168 | tf_op jit(solution)/shard_map/all_gather | solution.py:184
  191.2 4.3 reshape.487
  202.0 95.5 %while.32 = (s32[]{:T(128)}, bf16[4,128,1280]{1,2,0:T(8,128)(2,1)}, bf16[4,18,128,256]{3,2,1,0:T(8,128)(2,1)}, pred[4,128,2304]{2,1,0:T(8,128)(4,1)}, bf16[4,128...) while((s32[]{:T(128)}, bf16[4,128,1280]{1,2,0:T(8,128)(2,1)}, ...), condition=%wide.region_7.8_spmd, body=%wide.region_4.0_spmd.sunk | while | flops 1530759424 | bytes 38250596 | solution.py:230
  207.8 10.7 %fusion.123 = (f32[2,128,5]{1,2,0:T(8,128)S(1)}, f32[2,128,5,2304]{3,1,2,0:T(8,128)}) fusion(pred[128,2304]{1,0:T(8,128)(4,1)} %dynamic-slice_bitcast_fusion.5, bf16[128,2,5,128]{0,3,2,1:T(8,128)(2,1)} %bitcast.225, bf16[2304,2,128,1]{2,1,0,3:T(2,128)(2,1)S(1)} %bitcast.217), kind=kOutput, calls=%fused_computation.159.clone.1 | convolution fusion | flops 769722624 | bytes 13603840 | tf_op jit(solution)/shard_map/while/body/eval_jaxpr/sub | solution.py:34
  218.8 6.4 fusion.124
  231.6 10.7 %fusion.123 = (f32[2,128,5]{1,2,0:T(8,128)S(1)}, f32[2,128,5,2304]{3,1,2,0:T(8,128)}) fusion(pred[128,2304]{1,0:T(8,128)(4,1)} %dynamic-slice_bitcast_fusion.5, bf16[128,2,5,128]{0,3,2,1:T(8,128)(2,1)} %bitcast.225, bf16[2304,2,128,1]{2,1,0,3:T(2,128)(2,1)S(1)} %bitcast.217), kind=kOutput, calls=%fused_computation.159.clone.1 | convolution fusion | flops 769722624 | bytes 13603840 | tf_op jit(solution)/shard_map/while/body/eval_jaxpr/sub | solution.py:34
  242.5 6.5 fusion.124
  255.3 10.9 %fusion.123 = (f32[2,128,5]{1,2,0:T(8,128)S(1)}, f32[2,128,5,2304]{3,1,2,0:T(8,128)}) fusion(pred[128,2304]{1,0:T(8,128)(4,1)} %dynamic-slice_bitcast_fusion.5, bf16[128,2,5,128]{0,3,2,1:T(8,128)(2,1)} %bitcast.225, bf16[2304,2,128,1]{2,1,0,3:T(2,128)(2,1)S(1)} %bitcast.217), kind=kOutput, calls=%fused_computation.159.clone.1 | convolution fusion | flops 769722624 | bytes 13603840 | tf_op jit(solution)/shard_map/while/body/eval_jaxpr/sub | solution.py:34
  266.5 6.5 fusion.124
  279.3 10.7 %fusion.123 = (f32[2,128,5]{1,2,0:T(8,128)S(1)}, f32[2,128,5,2304]{3,1,2,0:T(8,128)}) fusion(pred[128,2304]{1,0:T(8,128)(4,1)} %dynamic-slice_bitcast_fusion.5, bf16[128,2,5,128]{0,3,2,1:T(8,128)(2,1)} %bitcast.225, bf16[2304,2,128,1]{2,1,0,3:T(2,128)(2,1)S(1)} %bitcast.217), kind=kOutput, calls=%fused_computation.159.clone.1 | convolution fusion | flops 769722624 | bytes 13603840 | tf_op jit(solution)/shard_map/while/body/eval_jaxpr/sub | solution.py:34
  290.2 6.5 fusion.124
  299.9 20.7 %all-gather.9.cloned.1.call-done = bf16[1280,2560]{0,1:T(8,128)(2,1)} async-done(((bf16[1280,320]{0,1:T(8,128)(2,1)}), bf16[1280,2560]{0,1:T(8,128)(2,1)}) %all-gather.9.cloned.1.call-update) | async-done | bytes 6553616 | tf_op jit(solution)/shard_map/all_gather | solution.py:235
  320.6 8.3 convolution_convert_fusion.10
  328.9 252.5 %while.33 = (s32[]{:T(128)}, bf16[4,128,1280]{2,1,0:T(8,128)(2,1)}, f32[4,18,32768]{2,1,0:T(8,128)}, f32[4,18,32768]{2,1,0:T(8,128)}, bf16[4,18,128,256]{3,2,1,0...) while((s32[]{:T(128)}, bf16[4,128,1280]{2,1,0:T(8,128)(2,1)}, ...), condition=%wide.region_12.13_spmd, body=%wide.region_9.12_spmd.sunk | while | flops 3811083264 | bytes 134538416 | solution.py:247
  336.8 8.3 fusion.136
  347.5 7.6 multiply_convert_fusion.2
  360.4 5.2 fusion.137
  365.6 3.2 copy.208
  368.8 3.6 broadcast_in_dim.169
  372.4 5.2 convolution_bitcast_fusion.2
  377.6 4.9 copy.209
  382.6 4.8 broadcast_in_dim.170
  387.3 4.9 constant_dynamic-update-slice_fusion.25
  399.7 8.3 fusion.136
  410.5 7.6 multiply_convert_fusion.2
  423.3 5.2 fusion.137
  431.7 3.6 broadcast_in_dim.169
  435.3 5.2 convolution_bitcast_fusion.2
  440.6 4.9 copy.209
  445.5 4.8 broadcast_in_dim.170
  450.2 4.9 constant_dynamic-update-slice_fusion.25
  462.6 8.3 fusion.136
  473.4 7.6 multiply_convert_fusion.2
  486.3 5.2 fusion.137
  494.7 3.6 broadcast_in_dim.169
  498.3 5.2 convolution_bitcast_fusion.2
  503.5 4.9 copy.209
  508.4 4.8 broadcast_in_dim.170
  513.2 5.1 constant_dynamic-update-slice_fusion.25
  525.7 8.3 fusion.136
  536.5 7.6 multiply_convert_fusion.2
  549.4 5.2 fusion.137
  557.8 3.6 broadcast_in_dim.169
  561.4 5.2 convolution_bitcast_fusion.2
  566.6 4.9 copy.209
  571.5 4.8 broadcast_in_dim.170
  576.3 4.9 constant_dynamic-update-slice_fusion.25
  584.0 14.2 %copy.134 = f32[4,18,32768]{2,0,1:T(4,128)} copy(f32[4,18,32768]{2,1,0:T(8,128)} %get-tuple-element.188) | data formatting | bytes 18874368 | tf_op jit(solution)/shard_map/while | solution.py:247
  598.2 7.2 slice.345
  608.1 14.5 %copy.139 = f32[4,18,32768]{2,0,1:T(4,128)} copy(f32[4,18,32768]{2,1,0:T(8,128)} %get-tuple-element.189) | data formatting | bytes 18874368 | tf_op jit(solution)/shard_map/while | solution.py:247
  622.6 7.5 slice.344
  630.1 7.7 convolution_convert_fusion.9
  637.8 4.5 copy.170
  661.2 4.0 reshape.496
  665.2 5.5 all-to-all-start.1
  679.9 4.1 reshape.503
  686.9 84.2 %all-to-all-done.1 = bf16[8,6,32768]{2,1,0:T(8,128)(2,1)} async-done(((bf16[8,6,32768]{2,1,0:T(8,128)(2,1)}), bf16[8,6,32768]{2,1,0:T(8,128)(2,1)}, u32[]{:S(2)}, u32[]{:S(2)}) %all-to-all-start.1) | async-done | bytes 3145760 | tf_op jit(solution)/shard_map/all_to_all | solution.py:309
  771.2 4.6 all-to-all-start.2
  780.9 76.7 %all-reduce.10.cloned.1.call-done = (bf16[4,32768]{1,0:T(4,128)(2,1)}, bf16[4,32768]{1,0:T(4,128)(2,1)}) async-done(((bf16[4,32768]{1,0:T(4,128)(2,1)}, bf16[4,32768]{1,0:T(4,128)(2,1)}), (bf16[4,32768]{1,0:T(4,128)(2,1)}, bf16[4,32768]{1,0:T(4,128)(2,1)})) %all-reduce.10.cloned.1.call-update) | async-done | bytes 524304 | tf_op jit(solution)/shard_map/psum | solution.py:285
  862.6 31.7 %reduce-scatter.4.cloned.1.call-done = bf16[640,512]{1,0:T(8,128)(2,1)} async-done(((bf16[2560,512]{1,0:T(8,128)(2,1)}), bf16[640,512]{1,0:T(8,128)(2,1)}) %reduce-scatter.4.cloned.1.call-update) | async-done | bytes 655376
  (263 shorter events, 203.1 us)
Async XLA Ops:
  7.2 83.8 %all-reduce.12.cloned.1.call-start = ((), (), s32[]{:S(2)}) async-start(), calls=%async_computation.10 | async-start | bytes 1048576 | tf_op jit(solution)/shard_map/psum | solution.py:153
  9.1 3.9 copy-start.17
  9.9 21.5 %copy-start.15 = (s32[4]{0:T(128)}, s32[4]{0:T(128)S(1)}, u32[]{:S(2)}) copy-start(s32[4]{0:T(128)S(1)} %dynamic_slice.39) | copy-start | bytes 52
  11.0 4.1 copy-start.4
  11.0 10.4 %copy-start.5 = (bf16[512,256]{1,0:T(8,128)(2,1)S(1)}, bf16[512,256]{1,0:T(8,128)(2,1)}, u32[]{:S(2)}) copy-start(bf16[512,256]{1,0:T(8,128)(2,1)} %param.31) | copy-start | bytes 786436
  11.1 13.2 %copy-start.11 = (s32[4,12]{1,0:T(4,128)S(1)}, s32[4,12]{1,0:T(4,128)}, u32[]{:S(2)}) copy-start(s32[4,12]{1,0:T(4,128)} %param.38) | copy-start | bytes 580
  11.1 13.3 %copy-start.20 = (s32[48,1]{0,1:T(1,128)S(1)}, s32[48,1]{0,1:T(1,128)}, u32[]{:S(2)}) copy-start(s32[48,1]{0,1:T(1,128)} %param.37) | copy-start | bytes 580
  12.1 18.7 %copy-start.21 = (s32[32]{0:T(128)S(1)}, s32[32]{0:T(128)}, u32[]{:S(2)}) copy-start(s32[32]{0:T(128)} %param.35) | copy-start | bytes 388
  12.1 18.9 %copy-start.22 = (s32[4]{0:T(128)S(1)}, s32[4]{0:T(128)}, u32[]{:S(2)}) copy-start(s32[4]{0:T(128)} %param.36) | copy-start | bytes 52
  12.1 19.0 %copy-start.19 = (s32[4,12]{1,0:T(4,128)S(1)}, s32[4,12]{1,0:T(4,128)}, u32[]{:S(2)}) copy-start(s32[4,12]{1,0:T(4,128)} %param.39) | copy-start | bytes 580
  13.1 128.3 %all-gather.5.cloned.1.call-start = ((), (), s32[]{:S(2)}) async-start(), calls=%async_computation.4 | async-start | bytes 2359296 | tf_op jit(solution)/shard_map/all_gather | solution.py:185
  13.8 177.3 %all-gather.7.cloned.1.call-start = ((), (), s32[]{:S(2)}) async-start(), calls=%async_computation.5 | async-start | bytes 2359296 | tf_op jit(solution)/shard_map/all_gather | solution.py:184
  14.6 285.3 %all-gather.11.cloned.1.call-start = ((), (), s32[]{:S(2)}) async-start(), calls=%async_computation.7 | async-start | bytes 3276800 | tf_op jit(solution)/shard_map/all_gather | solution.py:232
  15.9 22.4 %collective-permute-start = (bf16[384,256]{1,0:T(8,128)(2,1)}, bf16[384,256]{1,0:T(8,128)(2,1)}, u32[]{:S(2)}, u32[]{:S(2)}) collective-permute-start(bf16[384,256]{1,0:T(8,128)(2,1)} %slice.240), channel_id=1, source_target_pairs={{0,4},{4,8},{8,12},{12,16},{16,20},{20,24},{24,28},{1,5},{5,9},{9,... | collective-permute-start | bytes 589832 | tf_op jit(solution)/shard_map/ppermute | solution.py:17
  21.4 18.6 %collective-permute-start.1 = (bf16[384,256]{1,0:T(8,128)(2,1)S(1)}, bf16[384,256]{1,0:T(8,128)(2,1)S(1)}, u32[]{:S(2)}, u32[]{:S(2)}) collective-permute-start(bf16[384,256]{1,0:T(8,128)(2,1)S(1)} %slice.248), channel_id=1, source_target_pairs={{0,4},{4,8},{8,12},{12,16},{16,20},{20,24},{24,28},{1,5},{5,9},{9,... | collective-permute-start | bytes 589832 | tf_op jit(solution)/shard_map/ppermute | solution.py:17
  24.6 0.8 copy-start.12
  25.4 12.2 %all-to-all-start = ((s32[8,1,6]{2,1,0:T(1,128)}), s32[8,1,6]{2,1,0:T(1,128)S(1)}, u32[]{:S(2)}, u32[]{:S(2)}) async-start(s32[8,1,6]{2,1,0:T(1,128)} %bitcast.52), calls=%async_computation | async-start | bytes 8192 | tf_op jit(solution)/shard_map/all_to_all | solution.py:181
  30.2 290.4 %all-gather.9.cloned.1.call-start = ((), (), s32[]{:S(2)}) async-start(), calls=%async_computation.6 | async-start | bytes 7372800 | tf_op jit(solution)/shard_map/all_gather | solution.py:235
  32.5 59.9 %copy-start.9 = (s32[8]{0:T(128)}, s32[8]{0:T(128)S(1)}, u32[]{:S(2)}) copy-start(s32[8]{0:T(128)S(1)} %eq.130) | copy-start | bytes 100
  355.1 2.5 copy-start
  418.1 2.5 copy-start
  481.0 2.5 copy-start
  544.1 2.5 copy-start
  622.6 7.5 copy-start.8
  637.8 5.2 copy-start.10
  653.5 1.0 copy-start.3
  653.5 4.9 copy-start.13
  654.4 244.9 %collective-permute-start.2 = (bf16[3,32768]{1,0:T(4,128)(2,1)S(1)}, bf16[3,32768]{1,0:T(4,128)(2,1)}, u32[]{:S(2)}, u32[]{:S(2)}) collective-permute-start(bf16[3,32768]{1,0:T(4,128)(2,1)S(1)} %slice.347), channel_id=1, source_target_pairs={{4,0},{8,4},{12,8},{16,12},{20,16},{24,20},{28,24},{5,1},{9,5},{13... | collective-permute-start | bytes 589832 | tf_op jit(solution)/shard_map/ppermute | solution.py:17
  665.2 106.0 %all-to-all-start.1 = ((bf16[8,6,32768]{2,1,0:T(8,128)(2,1)}), bf16[8,6,32768]{2,1,0:T(8,128)(2,1)}, u32[]{:S(2)}, u32[]{:S(2)}) async-start(bf16[8,6,32768]{2,1,0:T(8,128)(2,1)} %reshape.496), calls=%async_computation.1 | async-start | bytes 8388608 | tf_op jit(solution)/shard_map/all_to_all | solution.py:309
  670.7 186.8 %all-reduce.10.cloned.1.call-start = ((), (), s32[]{:S(2)}) async-start(), calls=%async_computation.9 | async-start | bytes 1048576 | tf_op jit(solution)/shard_map/psum | solution.py:285
  671.3 223.0 %reduce-scatter.4.cloned.1.call-start = ((), (), s32[]{:S(2)}) async-start(), calls=%async_computation.8 | async-start | bytes 3276800
  672.4 0.8 copy-start.6
  679.9 4.1 copy-start.7
  679.9 5.3 copy-start.1
  686.9 170.6 %copy-start.16 = (s32[4]{0:T(128)S(1)}, s32[4]{0:T(128)}, u32[]{:S(2)}) copy-start(s32[4]{0:T(128)} %copy-done.15) | copy-start | bytes 52
  686.9 170.6 %copy-start.18 = (f32[4]{0:T(128)S(1)}, f32[4]{0:T(128)}, u32[]{:S(2)}) copy-start(f32[4]{0:T(128)} %copy-done.17) | copy-start | bytes 52
  771.2 131.5 %all-to-all-start.2 = ((bf16[8,6,32768]{2,1,0:T(8,128)(2,1)}), bf16[8,6,32768]{2,1,0:T(8,128)(2,1)}, u32[]{:S(2)}, u32[]{:S(2)}) async-start(bf16[8,6,32768]{2,1,0:T(8,128)(2,1)} %reshape.503), calls=%async_computation.2 | async-start | bytes 8388608 | tf_op jit(solution)/shard_map/all_to_all | solution.py:310
  778.7 115.7 %copy-start.2 = (f32[7,32768]{1,0:T(8,128)}, f32[7,32768]{1,0:T(8,128)S(1)}, u32[]{:S(2)}) copy-start(f32[7,32768]{1,0:T(8,128)S(1)} %scatter-add.29) | copy-start | bytes 2752516
  779.6 125.9 %collective-permute-start.3 = (bf16[3,32768]{1,0:T(4,128)(2,1)}, bf16[3,32768]{1,0:T(4,128)(2,1)}, u32[]{:S(2)}, u32[]{:S(2)}) collective-permute-start(bf16[3,32768]{1,0:T(4,128)(2,1)} %slice.346), channel_id=1, source_target_pairs={{4,0},{8,4},{12,8},{16,12},{20,16},{24,20},{28,24},{5,1},{9,5},{13... | collective-permute-start | bytes 589832 | tf_op jit(solution)/shard_map/ppermute | solution.py:17
  894.3 5.0 copy-start.14
Sparse Core Ops, SparseCore 0:
  13.2 77.6 all-reduce.11
  93.1 48.2 all-gather.4
  143.5 47.6 all-gather.6
  192.6 24.0 all-gather.10
  218.7 101.8 all-gather.8
  675.3 182.2 all-reduce.9
  860.1 34.2 reduce-scatter.3
where the time goes:
time: 927 us; the launch traced here: 916 us
  waiting for transfers between devices  353 us (38%)
  local copies, waits for them, and re-layouts  290 us (31%)
  matrix products  224 us (24%)
  starting transfers between devices  26.1 us (3%)
  between operations  15.2 us (2%)
    dot_general x20, matrix products, product(): return jnp.einsum(form, left, right, preferred_element_type=jnp.float32)  105 us
    all_to_all x1, waiting for transfers between devices, on_device(): lax.all_to_all(slot_dk, 'seq', split_axis=0, concat_axis=0, tiled=True)  84.2 us
    psum x1, waiting for transfers between devices, on_device(): lax.psum(section_dk.astype(jnp.bfloat16), 'seq').astype(jnp.float32)  76.7 us
    sub x8, matrix products, softmax_weights(): exponent = jnp.where(allowed, jnp.exp(masked - row_max), 0.0)  75.9 us
    all_gather x1, waiting for transfers between devices, on_device(): lax.all_gather(values, 'seq', axis=0, tiled=True)  45.9 us
    psum x1, waiting for transfers between devices, on_device(): lax.psum(part_values.astype(jnp.bfloat16), 'seq').astype(jnp.float32)  45.7 us
    all_gather x1, waiting for transfers between devices, on_device(): lax.all_gather(keys, 'seq', axis=0, tiled=True)  45.1 us
    dynamic_slice x32, local copies, waits for them, and re-layouts, on_device(): lax.map(run_forward, (query_blocks, key_sets, value_sets, allowed))  37.7 us
  transfers between devices with their start and end apart: 14, of which 7 were waited for; matrix products, arithmetic and copies ran while one was open for 19% of the time, Pallas kernels for 0%

commit v1 on v0

--- a/solution.py
+++ b/solution.py
@@ -282,7 +282,7 @@
         precision=lax.Precision.HIGHEST,
     )
     summed_dk, summed_dv = (
-        lax.psum(section_dk.astype(jnp.bfloat16), "seq").astype(jnp.float32),
+        jnp.sum(lax.all_gather(section_dk.astype(jnp.bfloat16), "seq"), axis=0).astype(jnp.float32),
         lax.psum(section_dv.astype(jnp.bfloat16), "seq").astype(jnp.float32),
     )
     spread_down = (mine / root_counts[:, None]).T

time: 927 us -> 964 us (1.040)
  waiting for transfers between devices: 353 us -> 384 us
    all_gather x0 -> x1, waiting for transfers between devices: none -> 89.9 us  [on_device(): lax.all_gather(section_dk.astype(jnp.bfloat16), 'seq')]
    psum x1, waiting for transfers between devices: 76.7 us -> 22.9 us  [on_device(): lax.psum(section_dv.astype(jnp.bfloat16), 'seq').astype(jnp.float32)]
    unnamed x8 -> x9, waiting for transfers between devices: 34.7 us -> 34.7 us
  transfers between devices with their start and end apart: 14 -> 15, of which waited for: 7 -> 8; matrix products, arithmetic and copies ran while one was open for 19% -> 19% of each run, Pallas kernels for 0% -> 0%
where the time goes in v1:
time: 964 us; the launch traced here: 954 us
  waiting for transfers between devices  384 us (40%)
  local copies, waits for them, and re-layouts  294 us (30%)
  matrix products  224 us (23%)
  starting transfers between devices  26.3 us (3%)
  between operations  15.2 us (2%)
  other arithmetic  9.68 us (1%)
    dot_general x20, matrix products, product(): return jnp.einsum(form, left, right, preferred_element_type=jnp.float32)  105 us
    all_gather x1, waiting for transfers between devices, on_device(): lax.all_gather(section_dk.astype(jnp.bfloat16), 'seq')  89.9 us
    all_to_all x1, waiting for transfers between devices, on_device(): lax.all_to_all(slot_dk, 'seq', split_axis=0, concat_axis=0, tiled=True)  78.4 us
    sub x8, matrix products, softmax_weights(): exponent = jnp.where(allowed, jnp.exp(masked - row_max), 0.0)  76 us
    all_gather x1, waiting for transfers between devices, on_device(): lax.all_gather(values, 'seq', axis=0, tiled=True)  45.9 us
    psum x1, waiting for transfers between devices, on_device(): lax.psum(part_values.astype(jnp.bfloat16), 'seq').astype(jnp.float32)  45.8 us
    all_gather x1, waiting for transfers between devices, on_device(): lax.all_gather(keys, 'seq', axis=0, tiled=True)  45.1 us
    dynamic_slice x32, local copies, waits for them, and re-layouts, on_device(): lax.map(run_forward, (query_blocks, key_sets, value_sets, allowed))  37.7 us
  transfers between devices with their start and end apart: 15, of which 8 were waited for; matrix products, arithmetic and copies ran while one was open for 19% of the time, Pallas kernels for 0%

profile of v1, /device:TPU:0, one launch (start us, length us, event | category | flops | bytes accessed | tf_op | source)
XLA Modules:
  0.0 953.7 jit_solution(747044220377853183)
XLA Ops:
  15.9 5.5 collective-permute-start
  25.4 4.8 all-to-all-start
  45.1 45.8 %all-reduce.11.cloned.1.call-done = (bf16[4,32768]{1,0:T(4,128)(2,1)}, bf16[4,32768]{1,0:T(4,128)(2,1)}) async-done(((bf16[4,32768]{1,0:T(4,128)(2,1)}, bf16[4,32768]{1,0:T(4,128)(2,1)}), (bf16[4,32768]{1,0:T(4,128)(2,1)}, bf16[4,32768]{1,0:T(4,128)(2,1)})) %all-reduce.11.cloned.1.call-update) | async-done | bytes 524304 | tf_op jit(solution)/shard_map/psum | solution.py:153
  95.5 45.9 %all-gather.8.cloned.1.call-done = bf16[4096,256]{1,0:T(8,128)(2,1)} async-done(((bf16[512,256]{1,0:T(8,128)(2,1)}), bf16[4096,256]{1,0:T(8,128)(2,1)}) %all-gather.8.cloned.1.call-update) | async-done | bytes 2097168 | tf_op jit(solution)/shard_map/all_gather | solution.py:185
  146.0 45.1 %all-gather.10.cloned.1.call-done = bf16[4096,256]{1,0:T(8,128)(2,1)} async-done(((bf16[512,256]{1,0:T(8,128)(2,1)}), bf16[4096,256]{1,0:T(8,128)(2,1)}) %all-gather.10.cloned.1.call-update) | async-done | bytes 2097168 | tf_op jit(solution)/shard_map/all_gather | solution.py:184
  191.2 4.3 reshape.487
  202.0 95.4 %while.32 = (s32[]{:T(128)}, bf16[4,128,1280]{1,2,0:T(8,128)(2,1)}, bf16[4,18,128,256]{3,2,1,0:T(8,128)(2,1)}, pred[4,128,2304]{2,1,0:T(8,128)(4,1)}, bf16[4,128...) while((s32[]{:T(128)}, bf16[4,128,1280]{1,2,0:T(8,128)(2,1)}, ...), condition=%wide.region_7.8_spmd, body=%wide.region_4.0_spmd.sunk | while | flops 1530759424 | bytes 38250596 | solution.py:230
  207.8 10.7 %fusion.124 = (f32[2,128,5]{1,2,0:T(8,128)S(1)}, f32[2,128,5,2304]{3,1,2,0:T(8,128)}) fusion(pred[128,2304]{1,0:T(8,128)(4,1)} %dynamic-slice_bitcast_fusion.5, bf16[128,2,5,128]{0,3,2,1:T(8,128)(2,1)} %bitcast.227, bf16[2304,2,128,1]{2,1,0,3:T(2,128)(2,1)S(1)} %bitcast.219), kind=kOutput, calls=%fused_computation.160.clone.1 | convolution fusion | flops 769722624 | bytes 13603840 | tf_op jit(solution)/shard_map/while/body/eval_jaxpr/sub | solution.py:34
  218.7 6.4 fusion.125
  231.5 10.7 %fusion.124 = (f32[2,128,5]{1,2,0:T(8,128)S(1)}, f32[2,128,5,2304]{3,1,2,0:T(8,128)}) fusion(pred[128,2304]{1,0:T(8,128)(4,1)} %dynamic-slice_bitcast_fusion.5, bf16[128,2,5,128]{0,3,2,1:T(8,128)(2,1)} %bitcast.227, bf16[2304,2,128,1]{2,1,0,3:T(2,128)(2,1)S(1)} %bitcast.219), kind=kOutput, calls=%fused_computation.160.clone.1 | convolution fusion | flops 769722624 | bytes 13603840 | tf_op jit(solution)/shard_map/while/body/eval_jaxpr/sub | solution.py:34
  242.5 6.5 fusion.125
  255.2 10.9 %fusion.124 = (f32[2,128,5]{1,2,0:T(8,128)S(1)}, f32[2,128,5,2304]{3,1,2,0:T(8,128)}) fusion(pred[128,2304]{1,0:T(8,128)(4,1)} %dynamic-slice_bitcast_fusion.5, bf16[128,2,5,128]{0,3,2,1:T(8,128)(2,1)} %bitcast.227, bf16[2304,2,128,1]{2,1,0,3:T(2,128)(2,1)S(1)} %bitcast.219), kind=kOutput, calls=%fused_computation.160.clone.1 | convolution fusion | flops 769722624 | bytes 13603840 | tf_op jit(solution)/shard_map/while/body/eval_jaxpr/sub | solution.py:34
  266.5 6.5 fusion.125
  279.2 10.7 %fusion.124 = (f32[2,128,5]{1,2,0:T(8,128)S(1)}, f32[2,128,5,2304]{3,1,2,0:T(8,128)}) fusion(pred[128,2304]{1,0:T(8,128)(4,1)} %dynamic-slice_bitcast_fusion.5, bf16[128,2,5,128]{0,3,2,1:T(8,128)(2,1)} %bitcast.227, bf16[2304,2,128,1]{2,1,0,3:T(2,128)(2,1)S(1)} %bitcast.219), kind=kOutput, calls=%fused_computation.160.clone.1 | convolution fusion | flops 769722624 | bytes 13603840 | tf_op jit(solution)/shard_map/while/body/eval_jaxpr/sub | solution.py:34
  290.2 6.5 fusion.125
  299.8 20.8 %all-gather.12.cloned.1.call-done = bf16[1280,2560]{0,1:T(8,128)(2,1)} async-done(((bf16[1280,320]{0,1:T(8,128)(2,1)}), bf16[1280,2560]{0,1:T(8,128)(2,1)}) %all-gather.12.cloned.1.call-update) | async-done | bytes 6553616 | tf_op jit(solution)/shard_map/all_gather | solution.py:235
  320.6 8.3 convolution_convert_fusion.10
  328.9 252.4 %while.33 = (s32[]{:T(128)}, bf16[4,128,1280]{2,1,0:T(8,128)(2,1)}, f32[4,18,32768]{2,1,0:T(8,128)}, f32[4,18,32768]{2,1,0:T(8,128)}, bf16[4,18,128,256]{3,2,1,0...) while((s32[]{:T(128)}, bf16[4,128,1280]{2,1,0:T(8,128)(2,1)}, ...), condition=%wide.region_12.13_spmd, body=%wide.region_9.12_spmd.sunk | while | flops 3811083264 | bytes 134538416 | solution.py:247
  336.7 8.3 fusion.137
  347.5 7.6 multiply_convert_fusion.2
  360.4 5.2 fusion.138
  368.8 3.6 broadcast_in_dim.169
  372.4 5.2 convolution_bitcast_fusion.2
  377.6 4.9 copy.210
  382.5 4.8 broadcast_in_dim.170
  387.3 4.9 constant_dynamic-update-slice_fusion.25
  399.6 8.3 fusion.137
  410.4 7.6 multiply_convert_fusion.2
  423.3 5.2 fusion.138
  431.6 3.6 broadcast_in_dim.169
  435.3 5.2 convolution_bitcast_fusion.2
  440.5 4.9 copy.210
  445.4 4.8 broadcast_in_dim.170
  450.2 4.9 constant_dynamic-update-slice_fusion.25
  462.5 8.3 fusion.137
  473.3 7.6 multiply_convert_fusion.2
  486.2 5.2 fusion.138
  494.6 3.6 broadcast_in_dim.169
  498.2 5.2 convolution_bitcast_fusion.2
  503.4 4.9 copy.210
  508.3 4.8 broadcast_in_dim.170
  513.1 5.1 constant_dynamic-update-slice_fusion.25
  525.6 8.3 fusion.137
  536.4 7.6 multiply_convert_fusion.2
  549.3 5.2 fusion.138
  557.7 3.6 broadcast_in_dim.169
  561.3 5.2 convolution_bitcast_fusion.2
  566.5 4.9 copy.210
  571.4 4.8 broadcast_in_dim.170
  576.2 4.9 constant_dynamic-update-slice_fusion.25
  583.9 14.2 %copy.134 = f32[4,18,32768]{2,0,1:T(4,128)} copy(f32[4,18,32768]{2,1,0:T(8,128)} %get-tuple-element.188) | data formatting | bytes 18874368 | tf_op jit(solution)/shard_map/while | solution.py:247
  598.1 7.2 slice.345
  609.0 14.5 %copy.139 = f32[4,18,32768]{2,0,1:T(4,128)} copy(f32[4,18,32768]{2,1,0:T(8,128)} %get-tuple-element.189) | data formatting | bytes 18874368 | tf_op jit(solution)/shard_map/while | solution.py:247
  623.5 7.5 slice.344
  630.9 7.8 convolution_convert_fusion.9
  638.7 4.4 copy.170
  665.2 4.0 reshape.496
  669.2 5.6 all-to-all-start.1
  684.9 4.2 reshape.503
  692.1 78.4 %all-to-all-done.1 = bf16[8,6,32768]{2,1,0:T(8,128)(2,1)} async-done(((bf16[8,6,32768]{2,1,0:T(8,128)(2,1)}), bf16[8,6,32768]{2,1,0:T(8,128)(2,1)}, u32[]{:S(2)}, u32[]{:S(2)}) %all-to-all-start.1) | async-done | bytes 3145760 | tf_op jit(solution)/shard_map/all_to_all | solution.py:309
  770.5 4.5 all-to-all-start.2
  780.2 22.9 %all-reduce.9.cloned.1.call-done = bf16[4,32768]{1,0:T(4,128)(2,1)} async-done(((bf16[4,32768]{1,0:T(4,128)(2,1)}), bf16[4,32768]{1,0:T(4,128)(2,1)}) %all-reduce.9.cloned.1.call-update) | async-done | bytes 262160 | tf_op jit(solution)/shard_map/psum | solution.py:286
  805.7 89.9 %all-gather.16.cloned.1.call-done = bf16[8,4,32768]{2,1,0:T(4,128)(2,1)} async-done(((bf16[1,4,32768]{2,1,0:T(4,128)(2,1)}), bf16[8,4,32768]{2,1,0:T(4,128)(2,1)}) %all-gather.16.cloned.1.call-update) | async-done | bytes 2097168 | tf_op jit(solution)/shard_map/all_gather | solution.py:285
  899.7 32.2 %reduce-scatter.4.cloned.1.call-done = bf16[640,512]{1,0:T(8,128)(2,1)} async-done(((bf16[2560,512]{1,0:T(8,128)(2,1)}), bf16[640,512]{1,0:T(8,128)(2,1)}) %reduce-scatter.4.cloned.1.call-update) | async-done | bytes 655376
  (269 shorter events, 212.6 us)
Async XLA Ops:
  7.2 83.8 %all-reduce.11.cloned.1.call-start = ((), (), s32[]{:S(2)}) async-start(), calls=%async_computation.11 | async-start | bytes 1048576 | tf_op jit(solution)/shard_map/psum | solution.py:153
  9.1 3.9 copy-start.18
  9.9 21.5 %copy-start.16 = (s32[4]{0:T(128)}, s32[4]{0:T(128)S(1)}, u32[]{:S(2)}) copy-start(s32[4]{0:T(128)S(1)} %dynamic_slice.39) | copy-start | bytes 52
  11.0 4.1 copy-start.4
  11.0 10.4 %copy-start.5 = (bf16[512,256]{1,0:T(8,128)(2,1)S(1)}, bf16[512,256]{1,0:T(8,128)(2,1)}, u32[]{:S(2)}) copy-start(bf16[512,256]{1,0:T(8,128)(2,1)} %param.31) | copy-start | bytes 786436
  11.1 13.2 %copy-start.12 = (s32[4,12]{1,0:T(4,128)S(1)}, s32[4,12]{1,0:T(4,128)}, u32[]{:S(2)}) copy-start(s32[4,12]{1,0:T(4,128)} %param.38) | copy-start | bytes 580
  11.1 13.3 %copy-start.21 = (s32[48,1]{0,1:T(1,128)S(1)}, s32[48,1]{0,1:T(1,128)}, u32[]{:S(2)}) copy-start(s32[48,1]{0,1:T(1,128)} %param.37) | copy-start | bytes 580
  12.1 18.8 %copy-start.22 = (s32[32]{0:T(128)S(1)}, s32[32]{0:T(128)}, u32[]{:S(2)}) copy-start(s32[32]{0:T(128)} %param.35) | copy-start | bytes 388
  12.1 18.9 %copy-start.23 = (s32[4]{0:T(128)S(1)}, s32[4]{0:T(128)}, u32[]{:S(2)}) copy-start(s32[4]{0:T(128)} %param.36) | copy-start | bytes 52
  12.1 19.1 %copy-start.20 = (s32[4,12]{1,0:T(4,128)S(1)}, s32[4,12]{1,0:T(4,128)}, u32[]{:S(2)}) copy-start(s32[4,12]{1,0:T(4,128)} %param.39) | copy-start | bytes 580
  13.1 128.3 %all-gather.8.cloned.1.call-start = ((), (), s32[]{:S(2)}) async-start(), calls=%async_computation.4 | async-start | bytes 2359296 | tf_op jit(solution)/shard_map/all_gather | solution.py:185
  13.8 177.3 %all-gather.10.cloned.1.call-start = ((), (), s32[]{:S(2)}) async-start(), calls=%async_computation.5 | async-start | bytes 2359296 | tf_op jit(solution)/shard_map/all_gather | solution.py:184
  14.6 285.3 %all-gather.14.cloned.1.call-start = ((), (), s32[]{:S(2)}) async-start(), calls=%async_computation.7 | async-start | bytes 3276800 | tf_op jit(solution)/shard_map/all_gather | solution.py:232
  15.9 22.4 %collective-permute-start = (bf16[384,256]{1,0:T(8,128)(2,1)}, bf16[384,256]{1,0:T(8,128)(2,1)}, u32[]{:S(2)}, u32[]{:S(2)}) collective-permute-start(bf16[384,256]{1,0:T(8,128)(2,1)} %slice.240), channel_id=1, source_target_pairs={{0,4},{4,8},{8,12},{12,16},{16,20},{20,24},{24,28},{1,5},{5,9},{9,... | collective-permute-start | bytes 589832 | tf_op jit(solution)/shard_map/ppermute | solution.py:17
  21.4 18.6 %collective-permute-start.1 = (bf16[384,256]{1,0:T(8,128)(2,1)S(1)}, bf16[384,256]{1,0:T(8,128)(2,1)S(1)}, u32[]{:S(2)}, u32[]{:S(2)}) collective-permute-start(bf16[384,256]{1,0:T(8,128)(2,1)S(1)} %slice.248), channel_id=1, source_target_pairs={{0,4},{4,8},{8,12},{12,16},{16,20},{20,24},{24,28},{1,5},{5,9},{9,... | collective-permute-start | bytes 589832 | tf_op jit(solution)/shard_map/ppermute | solution.py:17
  24.6 0.8 copy-start.13
  25.4 12.2 %all-to-all-start = ((s32[8,1,6]{2,1,0:T(1,128)}), s32[8,1,6]{2,1,0:T(1,128)S(1)}, u32[]{:S(2)}, u32[]{:S(2)}) async-start(s32[8,1,6]{2,1,0:T(1,128)} %bitcast.53), calls=%async_computation | async-start | bytes 8192 | tf_op jit(solution)/shard_map/all_to_all | solution.py:181
  30.2 290.4 %all-gather.12.cloned.1.call-start = ((), (), s32[]{:S(2)}) async-start(), calls=%async_computation.6 | async-start | bytes 7372800 | tf_op jit(solution)/shard_map/all_gather | solution.py:235
  30.8 772.3 %all-reduce.9.cloned.1.call-start = ((), (), s32[]{:S(2)}) async-start(), calls=%async_computation.8 | async-start | bytes 524288 | tf_op jit(solution)/shard_map/psum | solution.py:286
  32.5 59.8 %copy-start.10 = (s32[8]{0:T(128)}, s32[8]{0:T(128)S(1)}, u32[]{:S(2)}) copy-start(s32[8]{0:T(128)S(1)} %eq.130) | copy-start | bytes 100
  355.1 2.5 copy-start
  418.0 2.5 copy-start
  480.9 2.5 copy-start
  544.0 2.5 copy-start
  623.5 7.5 copy-start.9
  651.8 1.0 copy-start.3
  652.8 7.0 copy-start.11
  652.8 9.6 %copy-start.14 = (s32[48]{0:T(128)S(1)}, s32[48]{0:T(128)}, u32[]{:S(2)}) copy-start(s32[48]{0:T(128)} %copy-done.13) | copy-start | bytes 580
  652.8 284.2 %collective-permute-start.2 = (bf16[3,32768]{1,0:T(4,128)(2,1)S(1)}, bf16[3,32768]{1,0:T(4,128)(2,1)}, u32[]{:S(2)}, u32[]{:S(2)}) collective-permute-start(bf16[3,32768]{1,0:T(4,128)(2,1)S(1)} %slice.347), channel_id=1, source_target_pairs={{4,0},{8,4},{12,8},{16,12},{20,16},{24,20},{28,24},{5,1},{9,5},{13... | collective-permute-start | bytes 589832 | tf_op jit(solution)/shard_map/ppermute | solution.py:17
  669.2 5.7 copy-start.8
  669.2 101.3 %all-to-all-start.1 = ((bf16[8,6,32768]{2,1,0:T(8,128)(2,1)}), bf16[8,6,32768]{2,1,0:T(8,128)(2,1)}, u32[]{:S(2)}, u32[]{:S(2)}) async-start(bf16[8,6,32768]{2,1,0:T(8,128)(2,1)} %reshape.496), calls=%async_computation.1 | async-start | bytes 8388608 | tf_op jit(solution)/shard_map/all_to_all | solution.py:309
  674.8 220.7 %all-gather.16.cloned.1.call-start = ((), (), s32[]{:S(2)}) async-start(), calls=%async_computation.9 | async-start | bytes 2359296 | tf_op jit(solution)/shard_map/all_gather | solution.py:285
  676.3 255.6 %reduce-scatter.4.cloned.1.call-start = ((), (), s32[]{:S(2)}) async-start(), calls=%async_computation.10 | async-start | bytes 3276800
  677.5 0.8 copy-start.6
  684.9 4.2 copy-start.7
  684.9 5.5 copy-start.1
  692.1 111.0 %copy-start.17 = (s32[4]{0:T(128)S(1)}, s32[4]{0:T(128)}, u32[]{:S(2)}) copy-start(s32[4]{0:T(128)} %copy-done.16) | copy-start | bytes 52
  692.1 111.0 %copy-start.19 = (f32[4]{0:T(128)S(1)}, f32[4]{0:T(128)}, u32[]{:S(2)}) copy-start(f32[4]{0:T(128)} %copy-done.18) | copy-start | bytes 52
  770.5 169.8 %all-to-all-start.2 = ((bf16[8,6,32768]{2,1,0:T(8,128)(2,1)}), bf16[8,6,32768]{2,1,0:T(8,128)(2,1)}, u32[]{:S(2)}, u32[]{:S(2)}) async-start(bf16[8,6,32768]{2,1,0:T(8,128)(2,1)} %reshape.503), calls=%async_computation.2 | async-start | bytes 8388608 | tf_op jit(solution)/shard_map/all_to_all | solution.py:310
  778.0 154.0 %copy-start.2 = (f32[7,32768]{1,0:T(8,128)}, f32[7,32768]{1,0:T(8,128)S(1)}, u32[]{:S(2)}) copy-start(f32[7,32768]{1,0:T(8,128)S(1)} %scatter-add.29) | copy-start | bytes 2752516
  778.9 164.3 %collective-permute-start.3 = (bf16[3,32768]{1,0:T(4,128)(2,1)}, bf16[3,32768]{1,0:T(4,128)(2,1)}, u32[]{:S(2)}, u32[]{:S(2)}) collective-permute-start(bf16[3,32768]{1,0:T(4,128)(2,1)} %slice.346), channel_id=1, source_target_pairs={{4,0},{8,4},{12,8},{16,12},{20,16},{24,20},{28,24},{5,1},{9,5},{13... | collective-permute-start | bytes 589832 | tf_op jit(solution)/shard_map/ppermute | solution.py:17
  932.0 5.0 copy-start.15
Sparse Core Ops, SparseCore 0:
  13.2 77.6 all-reduce.10
  93.1 48.2 all-gather.7
  143.5 47.6 all-gather.9
  192.6 24.0 all-gather.13
  218.7 101.8 all-gather.11
  662.5 140.5 all-reduce.8
  805.8 89.6 all-gather.15
  898.1 33.8 reduce-scatter.3
